TPU v7x, 32 devices: a whole 2x2x4 slice. The times are simulated.
32 devices in a mesh: grp: 2 (over y), ia: 4 (over x, core), ja: 4 (over z).
Axes of the slice: x: 2, y: 2, z: 4, core: 2. Of those that a mesh axis runs over, the one named last changes fastest.
Arguments:
- amplitudes: float32 [16, 8, 160, 160], P(('grp', 'ia'), 'ja'), parts along dimension 0, may hold values from -3 to 3
- integrals: float32 [16, 8, 160, 160], P(('grp', 'ia'), 'ja'), parts along dimension 0, may hold values from -6 to 6
- row_intersection: float32 [16, 8, 8, 160, 160], P(('grp', 'ia'), 'ja'), parts along dimension 0, as said below
- column_intersection: float32 [16, 8, 8, 160, 160], P(('grp', 'ia'), 'ja'), parts along dimension 0, as said below
- row_tiles: int32 [16, 8], P(('grp', 'ia')), parts along dimension 0, may hold values from 0 to 7, as said below
- row_coupling: float32 [16, 8], P(('grp', 'ia')), parts along dimension 0, may hold values from 0.02 to 0.12
- row_counts: int32 [16], P(('grp', 'ia')), parts along dimension 0, may hold values from 1 to 8, as said below
- column_tiles: int32 [16, 8], P(('grp', 'ja')), parts along dimension 0, may hold values from 0 to 7, as said below
- column_coupling: float32 [16, 8], P(('grp', 'ja')), parts along dimension 0, may hold values from 0.02 to 0.12
- column_counts: int32 [16], P(('grp', 'ja')), parts along dimension 0, may hold values from 1 to 8, as said below
- virtual_energy: float32 [16, 8, 160], P(('grp', 'ia'), 'ja'), parts along dimension 0, may hold values from 0.5 to 3
- first_energy: float32 [16], P(('grp', 'ia')), parts along dimension 0, may hold values from -1.5 to -0.3
- second_energy: float32 [16], P(('grp', 'ja')), parts along dimension 0, may hold values from -1.5 to -0.3
Outputs:
- new_amplitudes: float32 [16, 8, 160, 160], P(('grp', 'ia'), 'ja'), parts along dimension 0
- last_residual: float32 [16, 8, 160, 160], P(('grp', 'ia'), 'ja'), parts along dimension 0
There are 2 independent parts, one for each index of `grp`. A program takes and returns all parts, laid end to end along the dimension named above; each array names one. Nothing has to cross between parts.
Inputs may be any that keep to these rules, and one draw needn't show every extreme that they name: `row_tiles`: each row holds 8 different first-fragment orbitals. `column_tiles`: each row holds 8 different second-fragment orbitals. `row_counts`: some orbital has all 8 slots live. `column_counts`: some orbital has all 8 slots live. `row_intersection`: identity plus an independent perturbation of full rank. `column_intersection`: identity plus an independent perturbation of full rank.
All inputs are finite; a program needn't handle non-finite values.
Results may differ from a plain program's by a relative error of at most 0.00017.
Values sent between devices are 32-bit elements; how exact they have to be, the bound alone decides.
No kernel may reach another device: no remote copies, remote signals or barrier semaphores. Data moves between devices by JAX's collectives and lax.ppermute only.
A program may use at most 128 MiB of HBM per device.

v0:
```python
import jax
import jax.numpy as jnp
from jax import lax
from jax.sharding import PartitionSpec as P

ITERS = 2


def sandwich(intersection, block):
    left = jnp.matmul(intersection, block, precision=lax.Precision.HIGHEST)
    return jnp.matmul(left, jnp.swapaxes(intersection, -1, -2), precision=lax.Precision.HIGHEST)


def coupled_sum(intersection, chosen, weight, counts, row_side):
    longest = jnp.max(counts)

    def one_slot(slot, total):
        over_slot = lax.dynamic_index_in_dim(intersection, slot, 2, keepdims=False)
        chosen_slot = lax.dynamic_index_in_dim(chosen, slot, 2, keepdims=False)
        weight_slot = lax.dynamic_index_in_dim(weight, slot, 1, keepdims=False)
        product = sandwich(over_slot, chosen_slot)
        if row_side:
            scaled = weight_slot[:, None, None, None] * product
        else:
            scaled = weight_slot[None, :, None, None] * product
        return total + scaled

    start = jnp.zeros(chosen.shape[:2] + chosen.shape[3:], jnp.float32)
    return lax.fori_loop(0, longest, one_slot, start)


def local(
    amplitudes,
    integrals,
    row_intersection,
    column_intersection,
    row_tiles,
    row_coupling,
    row_counts,
    column_tiles,
    column_coupling,
    column_counts,
    virtual_energy,
    first_energy,
    second_energy,
):
    denom = (
        virtual_energy[:, :, :, None]
        + virtual_energy[:, :, None, :]
        - first_energy[:, None, None, None]
        - second_energy[None, :, None, None]
    )
    slot_index = jnp.arange(row_tiles.shape[1], dtype=jnp.int32)
    row_weight = row_coupling * (slot_index[None, :] < row_counts[:, None]).astype(jnp.float32)
    column_weight = column_coupling * (slot_index[None, :] < column_counts[:, None]).astype(
        jnp.float32
    )
    current = amplitudes
    residual = jnp.zeros_like(amplitudes)
    for iteration in range(ITERS):
        gathered_rows = lax.all_gather(current, "ia", axis=0, tiled=True)
        gathered_columns = lax.all_gather(current, "ja", axis=1, tiled=True)
        row_chosen = jnp.swapaxes(gathered_rows[row_tiles], 1, 2)
        column_chosen = gathered_columns[:, column_tiles]
        row_term = coupled_sum(row_intersection, row_chosen, row_weight, row_counts, True)
        column_term = coupled_sum(
            column_intersection, column_chosen, column_weight, column_counts, False
        )
        residual = integrals + denom * current - row_term - column_term
        current = current - residual / denom
    return (current, residual)


def solution(mesh):
    placed = (
        P(("grp", "ia"), "ja", None, None),
        P(("grp", "ia"), "ja", None, None),
        P(("grp", "ia"), "ja", None, None, None),
        P(("grp", "ia"), "ja", None, None, None),
        P(("grp", "ia"), None),
        P(("grp", "ia"), None),
        P(("grp", "ia")),
        P(("grp", "ja"), None),
        P(("grp", "ja"), None),
        P(("grp", "ja")),
        P(("grp", "ia"), "ja", None),
        P(("grp", "ia")),
        P(("grp", "ja")),
    )
    return jax.shard_map(
        local,
        mesh=mesh,
        in_specs=placed,
        out_specs=(P(("grp", "ia"), "ja", None, None), P(("grp", "ia"), "ja", None, None)),
        check_vma=False,
    )
```

profile of v0, /device:TPU:16, one launch (start us, length us, event | category | flops | bytes accessed | tf_op | source)
XLA Modules:
  0.0 275.3 jit_solution(13624956626482143141)
XLA Ops:
  9.5 5.4 %copy.44 = f32[2,2,8,160,160]{4,3,1,0,2:T(8,128)} copy(f32[2,2,8,160,160]{4,3,2,1,0:T(8,128)} %param.23) | data formatting | bytes 6553600 | tf_op jit(solution)/shard_map/while | solution.py:29
  15.1 5.6 %copy.47 = f32[2,2,8,160,160]{4,3,1,0,2:T(8,128)} copy(f32[2,2,8,160,160]{4,3,2,1,0:T(8,128)} %param.24) | data formatting | bytes 6553600 | tf_op jit(solution)/shard_map/while | solution.py:29
  22.1 14.0 %all-gather.5.cloned.1.call-done = f32[8,2,160,160]{3,2,1,0:T(8,128)} async-done(((f32[2,2,160,160]{3,2,1,0:T(8,128)}), f32[8,2,160,160]{3,2,1,0:T(8,128)}) %all-gather.5.cloned.1.call-update) | async-done | bytes 1638416 | tf_op jit(solution)/shard_map/all_gather | solution.py:61
  36.2 5.0 %gather_fusion = f32[16,2,160,160]{3,2,1,0:T(8,128)} fusion(f32[8,2,160,160]{3,2,1,0:T(8,128)} %all-gather.5.cloned.1.call-done, s32[1024]{0:T(1024)S(1)} %pad_clamp_fusion.1), kind=kCustom, calls=%fused_computation | custom fusion | bytes 6553664 | tf_op jit(solution)/shard_map/gather | solution.py:63
  41.2 34.7 %while.40 = (s32[]{:T(128)}, f32[2,2,160,160]{3,2,1,0:T(8,128)S(1)}, s32[]{:T(128)}, f32[2,8]{0,1:T(8,128)S(1)}, f32[2,2,8,160,160]{4,3,1,0,2:T(8,128)}, /*index...) while((s32[]{:T(128)}, f32[2,2,160,160]{3,2,1,0:T(8,128)S(1)}, s32[]{:T(128)}, ...), condition=%wide.region_2.3_spmd, body=%wide.region_1.2_spmd.sunk | while | flops 393420800 | bytes 3605663 | solution.py:29
  41.9 2.1 fusion.79
  44.0 2.1 fusion.81
  46.8 2.1 fusion.79
  48.9 2.1 fusion.81
  51.7 2.1 fusion.79
  53.8 2.1 fusion.81
  56.5 2.1 fusion.79
  58.6 2.1 fusion.81
  61.4 2.1 fusion.79
  63.5 2.1 fusion.81
  66.2 2.1 fusion.79
  68.3 2.1 fusion.81
  71.1 2.1 fusion.79
  73.2 2.1 fusion.81
  75.9 15.4 %all-gather.7.cloned.1.call-done = f32[2,8,160,160]{3,2,1,0:T(8,128)} async-done(((f32[2,2,160,160]{3,2,1,0:T(8,128)}), f32[2,8,160,160]{3,2,1,0:T(8,128)}) %all-gather.7.cloned.1.call-update) | async-done | bytes 1638416 | tf_op jit(solution)/shard_map/all_gather | solution.py:62
  91.3 5.0 %gather_fusion.1 = f32[16,2,160,160]{3,2,1,0:T(8,128)} fusion(f32[2,8,160,160]{3,2,1,0:T(8,128)} %all-gather.7.cloned.1.call-done, s32[1024]{0:T(1024)S(1)} %pad_clamp_fusion), kind=kCustom, calls=%fused_computation.1 | custom fusion | bytes 6553664 | tf_op jit(solution)/shard_map/gather | solution.py:64
  96.4 39.2 %while.41 = (s32[]{:T(128)}, f32[2,2,160,160]{3,2,1,0:T(8,128)S(1)}, s32[]{:T(128)}, f32[2,8]{0,1:T(8,128)S(1)}, f32[2,2,8,160,160]{4,3,1,0,2:T(8,128)}, /*index...) while((s32[]{:T(128)}, f32[2,2,160,160]{3,2,1,0:T(8,128)S(1)}, s32[]{:T(128)}, ...), condition=%wide.region_5.6_spmd, body=%wide.region_4.5_spmd.sunk | while | flops 393420800 | bytes 3605663 | solution.py:29
  97.1 2.1 fusion.85
  99.2 2.1 fusion.87
  101.9 2.1 fusion.85
  104.0 2.1 fusion.87
  106.7 2.1 fusion.85
  108.8 2.1 fusion.87
  111.5 2.1 fusion.85
  113.6 2.1 fusion.87
  116.4 2.1 fusion.85
  118.4 2.1 fusion.87
  121.2 2.1 fusion.85
  123.2 2.1 fusion.87
  126.0 2.1 fusion.85
  128.0 2.1 fusion.87
  130.8 2.1 fusion.85
  132.8 2.1 fusion.87
  137.3 25.0 %all-gather.9.cloned.1.call-done = f32[8,2,160,160]{3,2,1,0:T(8,128)} async-done(((f32[2,2,160,160]{3,2,1,0:T(8,128)}), f32[8,2,160,160]{3,2,1,0:T(8,128)}) %all-gather.9.cloned.1.call-update) | async-done | bytes 1638416 | tf_op jit(solution)/shard_map/all_gather | solution.py:61
  162.3 4.9 %gather_fusion.2 = f32[16,2,160,160]{3,2,1,0:T(8,128)} fusion(f32[8,2,160,160]{3,2,1,0:T(8,128)} %all-gather.9.cloned.1.call-done, s32[1024]{0:T(1024)S(1)} %pad_clamp_fusion.1), kind=kCustom, calls=%fused_computation.2 | custom fusion | bytes 6553664 | tf_op jit(solution)/shard_map/gather | solution.py:63
  167.2 5.4 %copy.60 = f32[2,8,2,160,160]{4,3,2,0,1:T(8,128)} copy(f32[2,8,2,160,160]{4,3,2,1,0:T(8,128)} %bitcast.100) | data formatting | bytes 6553600 | tf_op jit(solution)/shard_map/gather | solution.py:63
  172.6 34.7 %while.42 = (s32[]{:T(128)}, f32[2,2,160,160]{3,2,1,0:T(8,128)S(1)}, s32[]{:T(128)}, f32[2,8]{0,1:T(8,128)S(1)}, f32[2,2,8,160,160]{4,3,1,0,2:T(8,128)}, /*index...) while((s32[]{:T(128)}, f32[2,2,160,160]{3,2,1,0:T(8,128)S(1)}, s32[]{:T(128)}, ...), condition=%wide.region_7.8_spmd, body=%wide.region_6.7_spmd.sunk | while | flops 393420800 | bytes 3605663 | solution.py:29
  173.3 2.1 fusion.92
  175.5 2.1 fusion.94
  180.3 2.1 fusion.94
  183.1 2.1 fusion.92
  185.2 2.1 fusion.94
  190.0 2.1 fusion.94
  194.9 2.1 fusion.94
  197.6 2.1 fusion.92
  199.7 2.1 fusion.94
  204.6 2.1 fusion.94
  207.3 10.6 %all-gather.11.cloned.1.call-done = f32[2,8,160,160]{3,2,1,0:T(8,128)} async-done(((f32[2,2,160,160]{3,2,1,0:T(8,128)}), f32[2,8,160,160]{3,2,1,0:T(8,128)}) %all-gather.11.cloned.1.call-update) | async-done | bytes 1638416 | tf_op jit(solution)/shard_map/all_gather | solution.py:62
  217.9 5.0 %gather_fusion.3 = f32[16,2,160,160]{3,2,1,0:T(8,128)} fusion(f32[2,8,160,160]{3,2,1,0:T(8,128)} %all-gather.11.cloned.1.call-done, s32[1024]{0:T(1024)S(1)} %pad_clamp_fusion), kind=kCustom, calls=%fused_computation.3 | custom fusion | bytes 6553664 | tf_op jit(solution)/shard_map/gather | solution.py:64
  222.8 5.4 %copy.59 = f32[2,8,2,160,160]{4,3,0,2,1:T(8,128)} copy(f32[2,8,2,160,160]{4,3,2,1,0:T(8,128)} %bitcast.101) | data formatting | bytes 6553600 | tf_op jit(solution)/shard_map/gather | solution.py:64
  228.3 39.1 %while.43 = (s32[]{:T(128)}, f32[2,2,160,160]{3,2,1,0:T(8,128)S(1)}, s32[]{:T(128)}, f32[2,8]{0,1:T(8,128)S(1)}, f32[2,2,8,160,160]{4,3,1,0,2:T(8,128)}, /*index...) while((s32[]{:T(128)}, f32[2,2,160,160]{3,2,1,0:T(8,128)S(1)}, s32[]{:T(128)}, ...), condition=%wide.region_9.10_spmd, body=%wide.region_8.9_spmd.sunk | while | flops 393420800 | bytes 3605663 | solution.py:29
  231.1 2.1 fusion.101
  235.9 2.1 fusion.101
  240.7 2.1 fusion.101
  245.5 2.1 fusion.101
  250.3 2.1 fusion.101
  255.1 2.1 fusion.101
  259.9 2.1 fusion.101
  264.7 2.1 fusion.101
  (90 shorter events, 32.0 us)
Async XLA Ops:
  7.2 29.0 %all-gather.5.cloned.1.call-start = ((), (), s32[]{:S(2)}) async-start(), calls=%async_computation | async-start | bytes 3276800 | tf_op jit(solution)/shard_map/all_gather | solution.py:61
  7.9 83.4 %all-gather.7.cloned.1.call-start = ((), (), s32[]{:S(2)}) async-start(), calls=%async_computation.1 | async-start | bytes 3276800 | tf_op jit(solution)/shard_map/all_gather | solution.py:62
  8.6 153.7 %all-gather.9.cloned.1.call-start = ((), (), s32[]{:S(2)}) async-start(), calls=%async_computation.2 | async-start | bytes 3276800 | tf_op jit(solution)/shard_map/all_gather | solution.py:61
  9.5 5.4 %copy-start.6 = (f32[2,8]{1,0:T(2,128)S(1)}, f32[2,8]{1,0:T(2,128)}, u32[]{:S(2)}) copy-start(f32[2,8]{1,0:T(2,128)} %param.26) | copy-start | bytes 196
  9.5 5.5 %copy-start.8 = (s32[2,8]{1,0:T(2,128)S(1)}, s32[2,8]{1,0:T(2,128)}, u32[]{:S(2)}) copy-start(s32[2,8]{1,0:T(2,128)} %param.28) | copy-start | bytes 196
  15.1 5.6 %copy-start.7 = (f32[2,8]{1,0:T(2,128)S(1)}, f32[2,8]{1,0:T(2,128)}, u32[]{:S(2)}) copy-start(f32[2,8]{1,0:T(2,128)} %param.29) | copy-start | bytes 196
  15.1 5.7 %copy-start.9 = (s32[2]{0:T(128)S(1)}, s32[2]{0:T(128)}, u32[]{:S(2)}) copy-start(s32[2]{0:T(128)} %param.27) | copy-start | bytes 28
  15.1 6.4 %copy-start.10 = (s32[2]{0:T(128)S(1)}, s32[2]{0:T(128)}, u32[]{:S(2)}) copy-start(s32[2]{0:T(128)} %param.30) | copy-start | bytes 28
  96.3 39.2 %copy-start.1 = (f32[2,2,160,160]{3,2,1,0:T(8,128)S(1)}, f32[2,2,160,160]{3,2,1,0:T(8,128)}, u32[]{:S(2)}) copy-start(f32[2,2,160,160]{3,2,1,0:T(8,128)} %param.21) | copy-start | bytes 1228804
  96.3 39.2 %copy-start.2 = (f32[2,2,160,160]{3,2,1,0:T(8,128)S(1)}, f32[2,2,160,160]{3,2,1,0:T(8,128)}, u32[]{:S(2)}) copy-start(f32[2,2,160,160]{3,2,1,0:T(8,128)} %param.22) | copy-start | bytes 1228804
  96.3 39.2 %copy-start.3 = (f32[2,2,160]{2,1,0:T(2,128)S(1)}, f32[2,2,160]{2,1,0:T(2,128)}, u32[]{:S(2)}) copy-start(f32[2,2,160]{2,1,0:T(2,128)} %param.31) | copy-start | bytes 7684
  96.4 39.2 %copy-start.4 = (f32[2]{0:T(128)S(1)}, f32[2]{0:T(128)}, u32[]{:S(2)}) copy-start(f32[2]{0:T(128)} %param.33) | copy-start | bytes 28
  96.4 39.2 %copy-start.5 = (f32[2]{0:T(128)S(1)}, f32[2]{0:T(128)}, u32[]{:S(2)}) copy-start(f32[2]{0:T(128)} %param.32) | copy-start | bytes 28
  136.8 81.1 %all-gather.11.cloned.1.call-start = ((), (), s32[]{:S(2)}) async-start(), calls=%async_computation.3 | async-start | bytes 3276800 | tf_op jit(solution)/shard_map/all_gather | solution.py:62
  228.3 39.2 %copy-start = (f32[2,2,160,160]{3,2,1,0:T(8,128)S(1)}, f32[2,2,160,160]{3,2,1,0:T(8,128)}, u32[]{:S(2)}) copy-start(f32[2,2,160,160]{3,2,1,0:T(8,128)} %divide_subtract_fusion.1) | copy-start | bytes 1228804
Sparse Core Ops, SparseCore 0:
  9.5 26.5 all-gather.4
  37.7 53.5 all-gather.6
  136.9 25.3 all-gather.8
  164.3 53.5 all-gather.10
where the time goes:
time: 278 us; the launch traced here: 275 us
  matrix products  123 us (44%)
  waiting for transfers between devices  66.9 us (24%)
  local copies, waits for them, and re-layouts  42.4 us (15%)
  loops' own time  24 us (9%)
  between operations  14 us (5%)
  other arithmetic  4.52 us (2%)
    dot_general x30, matrix products, sandwich(): left = jnp.matmul(intersection, block, precision=lax.Precision.HIGHEST)  61.7 us
    dot_general x30, matrix products, sandwich(): jnp.matmul(left, jnp.swapaxes(intersection, -1, -2), precision=lax.Precis...  61.7 us
    all_gather x2, waiting for transfers between devices, local(): gathered_rows = lax.all_gather(current, 'ia', axis=0, tiled=True)  39 us
    all_gather x2, waiting for transfers between devices, local(): gathered_columns = lax.all_gather(current, 'ja', axis=1, tiled=True)  26 us
    another operation x4, loops' own time, coupled_sum(): return lax.fori_loop(0, longest, one_slot, start)  24 us
    gather x3, local copies, waits for them, and re-layouts, local(): column_chosen = gathered_columns[:, column_tiles]  15.3 us
    gather x3, local copies, waits for them, and re-layouts, local(): row_chosen = jnp.swapaxes(gathered_rows[row_tiles], 1, 2)  15.2 us
    while x2, local copies, waits for them, and re-layouts, coupled_sum(): return lax.fori_loop(0, longest, one_slot, start)  11 us
  transfers between devices with their start and end apart: 4, of which 4 were waited for; matrix products, arithmetic and copies ran while one was open for 31% of the time, Pallas kernels for 0%

commit v1 on v0

--- a/solution.py
+++ b/solution.py
@@ -2,6 +2,7 @@
 import jax.numpy as jnp
 from jax import lax
 from jax.sharding import PartitionSpec as P
+from jax.lax import axis_index, ppermute, psum
 
 ITERS = 2
 
@@ -59,7 +60,16 @@
     residual = jnp.zeros_like(amplitudes)
     for iteration in range(ITERS):
         gathered_rows = lax.all_gather(current, "ia", axis=0, tiled=True)
-        gathered_columns = lax.all_gather(current, "ja", axis=1, tiled=True)
+        arr_next = psum(1, "ja")
+        w1, upper, local_now = (arr_next, axis_index("ja"), current.shape[1])
+        kept_arr, r2 = (current, 1)
+        while r2 < w1:
+            kept_arr = jnp.concatenate(
+                [kept_arr, ppermute(kept_arr, "ja", [(idx, (idx - r2) % w1) for idx in range(w1)])],
+                1,
+            )
+            r2 = 2 * r2
+        gathered_columns = jnp.roll(kept_arr, upper * local_now, 1)
         row_chosen = jnp.swapaxes(gathered_rows[row_tiles], 1, 2)
         column_chosen = gathered_columns[:, column_tiles]
         row_term = coupled_sum(row_intersection, row_chosen, row_weight, row_counts, True)

time: 278 us -> 348 us (1.25)
  the two profiles are of different devices: /device:TPU:16 before, /device:TPU:19 now
where the time goes in v1:
time: 348 us; the launch traced here: 345 us
  matrix products  131 us (38%)
  waiting for transfers between devices  116 us (33%)
  local copies, waits for them, and re-layouts  41 us (12%)
  loops' own time  26.3 us (8%)
  between operations  14.3 us (4%)
  other arithmetic  14 us (4%)
    ppermute x4, waiting for transfers between devices, local(): ppermute(kept_arr, 'ja', [(idx, (idx - r2) % w1) for idx in range(w1)])  116 us
    dot_general x32, matrix products, sandwich(): jnp.matmul(left, jnp.swapaxes(intersection, -1, -2), precision=lax.Precis...  65.7 us
    dot_general x32, matrix products, sandwich(): left = jnp.matmul(intersection, block, precision=lax.Precision.HIGHEST)  65.6 us
    another operation x4, loops' own time, coupled_sum(): return lax.fori_loop(0, longest, one_slot, start)  26.3 us
    gather x3, local copies, waits for them, and re-layouts, local(): row_chosen = jnp.swapaxes(gathered_rows[row_tiles], 1, 2)  15.3 us
    gather x3, local copies, waits for them, and re-layouts, local(): column_chosen = gathered_columns[:, column_tiles]  11.8 us
    while x2, local copies, waits for them, and re-layouts, coupled_sum(): return lax.fori_loop(0, longest, one_slot, start)  10.8 us
  transfers between devices with their start and end apart: 6, of which 4 were waited for; matrix products, arithmetic and copies ran while one was open for 30% of the time, Pallas kernels for 0%

profile of v1, /device:TPU:19, one launch (start us, length us, event | category | flops | bytes accessed | tf_op | source)
XLA Modules:
  0.0 344.9 jit_solution(16708857341460478957)
XLA Ops:
  7.9 15.2 %collective-permute-done = f32[2,2,160,160]{3,2,1,0:T(8,128)S(1)} collective-permute-done((f32[2,2,160,160]{3,2,1,0:T(8,128)}, f32[2,2,160,160]{3,2,1,0:T(8,128)S(1)}, u32[]{:S(2)}, u32[]{:S(2)}) %collective-permute-start) | collective-permute-done | bytes 409632 | tf_op jit(solution)/shard_map/ppermute | solution.py:68
  32.2 5.4 %copy.47 = f32[2,2,8,160,160]{4,3,1,0,2:T(8,128)} copy(f32[2,2,8,160,160]{4,3,2,1,0:T(8,128)} %param.26) | data formatting | bytes 6553600 | tf_op jit(solution)/shard_map/while | solution.py:30
  37.7 5.4 %copy.44 = f32[2,2,8,160,160]{4,3,1,0,2:T(8,128)} copy(f32[2,2,8,160,160]{4,3,2,1,0:T(8,128)} %param.25) | data formatting | bytes 6553600 | tf_op jit(solution)/shard_map/while | solution.py:30
  43.1 37.8 %collective-permute-done.1 = f32[2,4,160,160]{3,2,1,0:T(8,128)} collective-permute-done((f32[2,4,160,160]{3,2,1,0:T(8,128)S(1)}, f32[2,4,160,160]{3,2,1,0:T(8,128)}, u32[]{:S(2)}, u32[]{:S(2)}) %collective-permute-start.1) | collective-permute-done | bytes 819232 | tf_op jit(solution)/shard_map/ppermute | solution.py:68
  80.9 3.0 fusion.49
  83.9 3.2 gather_fusion.1
  87.2 39.4 %while.41 = (s32[]{:T(128)}, f32[2,2,160,160]{3,2,1,0:T(8,128)S(1)}, s32[]{:T(128)}, f32[2,8]{0,1:T(8,128)S(1)}, f32[2,2,8,160,160]{4,3,1,0,2:T(8,128)}, /*index...) while((s32[]{:T(128)}, f32[2,2,160,160]{3,2,1,0:T(8,128)S(1)}, s32[]{:T(128)}, ...), condition=%wide.region_5.7_spmd, body=%wide.region_4.6_spmd.sunk | while | flops 393420800 | bytes 3605663 | solution.py:30
  89.9 2.1 fusion.97
  92.7 2.1 fusion.95
  94.8 2.1 fusion.97
  97.5 2.1 fusion.95
  99.6 2.1 fusion.97
  104.5 2.1 fusion.97
  107.2 2.1 fusion.95
  109.3 2.1 fusion.97
  112.0 2.1 fusion.95
  114.1 2.1 fusion.97
  116.9 2.1 fusion.95
  119.0 2.1 fusion.97
  123.8 2.1 fusion.97
  126.6 5.0 %gather_fusion = f32[16,2,160,160]{3,2,1,0:T(8,128)} fusion(f32[8,2,160,160]{3,2,1,0:T(8,128)} %all-gather.3.cloned.1.call-done, s32[1024]{0:T(1024)S(1)} %pad_clamp_fusion.1), kind=kCustom, calls=%fused_computation | custom fusion | bytes 6553664 | tf_op jit(solution)/shard_map/gather | solution.py:73
  131.7 39.5 %while.40 = (s32[]{:T(128)}, f32[2,2,160,160]{3,2,1,0:T(8,128)S(1)}, s32[]{:T(128)}, f32[2,8]{0,1:T(8,128)S(1)}, f32[2,2,8,160,160]{4,3,1,0,2:T(8,128)}, /*index...) while((s32[]{:T(128)}, f32[2,2,160,160]{3,2,1,0:T(8,128)S(1)}, s32[]{:T(128)}, ...), condition=%wide.region_2.3_spmd, body=%wide.region_1.2_spmd.sunk | while | flops 393420800 | bytes 3605663 | solution.py:30
  134.5 2.1 fusion.91
  139.4 2.1 fusion.91
  144.2 2.1 fusion.91
  147.0 2.1 fusion.89
  149.1 2.1 fusion.91
  153.9 2.1 fusion.91
  158.8 2.1 fusion.91
  163.6 2.1 fusion.91
  168.5 2.1 fusion.91
  171.6 24.5 %collective-permute-done.2 = f32[2,2,160,160]{3,2,1,0:T(8,128)S(1)} collective-permute-done((f32[2,2,160,160]{3,2,1,0:T(8,128)S(1)}, f32[2,2,160,160]{3,2,1,0:T(8,128)S(1)}, u32[]{:S(2)}, u32[]{:S(2)}) %collective-permute-start.2) | collective-permute-done | bytes 409632 | tf_op jit(solution)/shard_map/ppermute | solution.py:68
  197.2 38.2 %collective-permute-done.3 = f32[2,4,160,160]{3,2,1,0:T(8,128)} collective-permute-done((f32[2,4,160,160]{3,2,1,0:T(8,128)S(1)}, f32[2,4,160,160]{3,2,1,0:T(8,128)}, u32[]{:S(2)}, u32[]{:S(2)}) %collective-permute-start.3) | collective-permute-done | bytes 819232 | tf_op jit(solution)/shard_map/ppermute | solution.py:68
  235.3 3.2 fusion.44
  238.5 3.1 gather_fusion.3
  241.6 5.4 %copy.59 = f32[2,8,2,160,160]{4,3,0,2,1:T(8,128)} copy(f32[2,8,2,160,160]{4,3,2,1,0:T(8,128)} %bitcast.100) | data formatting | bytes 6553600 | tf_op jit(solution)/shard_map/gather | solution.py:74
  247.1 39.5 %while.43 = (s32[]{:T(128)}, f32[2,2,160,160]{3,2,1,0:T(8,128)S(1)}, s32[]{:T(128)}, f32[2,8]{0,1:T(8,128)S(1)}, f32[2,2,8,160,160]{4,3,1,0,2:T(8,128)}, /*index...) while((s32[]{:T(128)}, f32[2,2,160,160]{3,2,1,0:T(8,128)S(1)}, s32[]{:T(128)}, ...), condition=%wide.region_9.11_spmd, body=%wide.region_8.10_spmd.sunk | while | flops 393420800 | bytes 3605663 | solution.py:30
  250.0 2.1 fusion.111
  254.9 2.1 fusion.111
  259.7 2.1 fusion.111
  264.5 2.1 fusion.111
  269.4 2.1 fusion.111
  274.2 2.1 fusion.111
  279.1 2.1 fusion.111
  283.9 2.1 fusion.111
  286.7 5.0 %gather_fusion.2 = f32[16,2,160,160]{3,2,1,0:T(8,128)} fusion(f32[8,2,160,160]{3,2,1,0:T(8,128)} %all-gather.5.cloned.1.call-done, s32[1024]{0:T(1024)S(1)} %pad_clamp_fusion.1), kind=kCustom, calls=%fused_computation.2 | custom fusion | bytes 6553664 | tf_op jit(solution)/shard_map/gather | solution.py:73
  291.6 5.4 %copy.60 = f32[2,8,2,160,160]{4,3,2,0,1:T(8,128)} copy(f32[2,8,2,160,160]{4,3,2,1,0:T(8,128)} %bitcast.101) | data formatting | bytes 6553600 | tf_op jit(solution)/shard_map/gather | solution.py:73
  297.1 39.5 %while.42 = (s32[]{:T(128)}, f32[2,2,160,160]{3,2,1,0:T(8,128)S(1)}, s32[]{:T(128)}, f32[2,8]{0,1:T(8,128)S(1)}, f32[2,2,8,160,160]{4,3,1,0,2:T(8,128)}, /*index...) while((s32[]{:T(128)}, f32[2,2,160,160]{3,2,1,0:T(8,128)S(1)}, s32[]{:T(128)}, ...), condition=%wide.region_7.9_spmd, body=%wide.region_6.8_spmd.sunk | while | flops 393420800 | bytes 3605663 | solution.py:30
  297.9 2.1 fusion.102
  300.0 2.1 fusion.104
  302.8 2.1 fusion.102
  304.8 2.1 fusion.104
  307.6 2.1 fusion.102
  309.7 2.1 fusion.104
  312.4 2.1 fusion.102
  314.5 2.1 fusion.104
  317.3 2.1 fusion.102
  319.4 2.1 fusion.104
  322.1 2.1 fusion.102
  324.2 2.1 fusion.104
  327.0 2.1 fusion.102
  329.1 2.1 fusion.104
  331.8 2.1 fusion.102
  333.9 2.1 fusion.104
  (101 shorter events, 50.0 us)
Async XLA Ops:
  7.2 119.4 %all-gather.3.cloned.1.call-start = ((), (), s32[]{:S(2)}) async-start(), calls=%async_computation | async-start | bytes 3276800 | tf_op jit(solution)/shard_map/all_gather | solution.py:62
  7.2 16.0 %collective-permute-start = (f32[2,2,160,160]{3,2,1,0:T(8,128)}, f32[2,2,160,160]{3,2,1,0:T(8,128)S(1)}, u32[]{:S(2)}, u32[]{:S(2)}) collective-permute-start(f32[2,2,160,160]{3,2,1,0:T(8,128)} %param.23), channel_id=1, source_target_pairs={{0,3},{1,0},{2,1},{3,2},{4,7},{5,4},{6,5},{7,6},{8,11},{9,8},{10,9... | collective-permute-start | bytes 1228808 | tf_op jit(solution)/shard_map/ppermute | solution.py:68
  7.9 278.8 %all-gather.5.cloned.1.call-start = ((), (), s32[]{:S(2)}) async-start(), calls=%async_computation.1 | async-start | bytes 3276800 | tf_op jit(solution)/shard_map/all_gather | solution.py:62
  23.2 14.4 %copy-start.6 = (f32[2,2,160,160]{3,2,1,0:T(8,128)}, f32[2,2,160,160]{3,2,1,0:T(8,128)S(1)}, u32[]{:S(2)}) copy-start(f32[2,2,160,160]{3,2,1,0:T(8,128)S(1)} %collective-permute-done) | copy-start | bytes 1228804
  24.6 56.3 %collective-permute-start.1 = (f32[2,4,160,160]{3,2,1,0:T(8,128)S(1)}, f32[2,4,160,160]{3,2,1,0:T(8,128)}, u32[]{:S(2)}, u32[]{:S(2)}) collective-permute-start(f32[2,4,160,160]{3,2,1,0:T(8,128)S(1)} %pad_maximum_fusion), channel_id=1, source_target_pairs={{0,2},{1,3},{2,0},{3,1},{4,6},{5,7},{6,4},{7,5},{8,10},{9,11},{10,... | collective-permute-start | bytes 2457608 | tf_op jit(solution)/shard_map/ppermute | solution.py:68
  37.7 43.2 %copy-start.2 = (f32[2,2,160,160]{3,2,1,0:T(8,128)S(1)}, f32[2,2,160,160]{3,2,1,0:T(8,128)}, u32[]{:S(2)}) copy-start(f32[2,2,160,160]{3,2,1,0:T(8,128)} %param.23) | copy-start | bytes 1228804
  131.6 39.6 %copy-start.3 = (f32[2,2,160,160]{3,2,1,0:T(8,128)S(1)}, f32[2,2,160,160]{3,2,1,0:T(8,128)}, u32[]{:S(2)}) copy-start(f32[2,2,160,160]{3,2,1,0:T(8,128)} %param.23) | copy-start | bytes 1228804
  131.6 39.6 %copy-start.4 = (f32[2,2,160,160]{3,2,1,0:T(8,128)S(1)}, f32[2,2,160,160]{3,2,1,0:T(8,128)}, u32[]{:S(2)}) copy-start(f32[2,2,160,160]{3,2,1,0:T(8,128)} %param.24) | copy-start | bytes 1228804
  131.6 39.6 %copy-start.8 = (f32[2,2,160]{2,1,0:T(2,128)S(1)}, f32[2,2,160]{2,1,0:T(2,128)}, u32[]{:S(2)}) copy-start(f32[2,2,160]{2,1,0:T(2,128)} %param.33) | copy-start | bytes 7684
  131.6 39.6 %copy-start.9 = (f32[2]{0:T(128)S(1)}, f32[2]{0:T(128)}, u32[]{:S(2)}) copy-start(f32[2]{0:T(128)} %param.35) | copy-start | bytes 28
  131.7 39.6 %copy-start.10 = (f32[2]{0:T(128)S(1)}, f32[2]{0:T(128)}, u32[]{:S(2)}) copy-start(f32[2]{0:T(128)} %param.34) | copy-start | bytes 28
  171.6 25.6 %copy-start = (f32[2,2,160,160]{3,2,1,0:T(8,128)}, f32[2,2,160,160]{3,2,1,0:T(8,128)S(1)}, u32[]{:S(2)}) copy-start(f32[2,2,160,160]{3,2,1,0:T(8,128)S(1)} %divide_subtract_fusion.1) | copy-start | bytes 1228804
  171.6 24.5 %collective-permute-start.2 = (f32[2,2,160,160]{3,2,1,0:T(8,128)S(1)}, f32[2,2,160,160]{3,2,1,0:T(8,128)S(1)}, u32[]{:S(2)}, u32[]{:S(2)}) collective-permute-start(f32[2,2,160,160]{3,2,1,0:T(8,128)S(1)} %divide_subtract_fusion.1), channel_id=1, source_target_pairs={{0,3},{1,0},{2,1},{3,2},{4,7},{5,4},{6,5},{7,6},{8,11},{9,8},{10,9... | collective-permute-start | bytes 1228808 | tf_op jit(solution)/shard_map/ppermute | solution.py:68
  196.1 0.8 copy-start.7
  197.0 38.3 %collective-permute-start.3 = (f32[2,4,160,160]{3,2,1,0:T(8,128)S(1)}, f32[2,4,160,160]{3,2,1,0:T(8,128)}, u32[]{:S(2)}, u32[]{:S(2)}) collective-permute-start(f32[2,4,160,160]{3,2,1,0:T(8,128)S(1)} %pad_maximum_fusion.1), channel_id=1, source_target_pairs={{0,2},{1,3},{2,0},{3,1},{4,6},{5,7},{6,4},{7,5},{8,10},{9,11},{10,... | collective-permute-start | bytes 2457608 | tf_op jit(solution)/shard_map/ppermute | solution.py:68
  297.1 39.6 %copy-start.1 = (f32[2,2,160,160]{3,2,1,0:T(8,128)S(1)}, f32[2,2,160,160]{3,2,1,0:T(8,128)}, u32[]{:S(2)}) copy-start(f32[2,2,160,160]{3,2,1,0:T(8,128)} %copy-done) | copy-start | bytes 1228804
  297.1 39.6 %copy-start.5 = (f32[2,2,160,160]{3,2,1,0:T(8,128)S(1)}, f32[2,2,160,160]{3,2,1,0:T(8,128)}, u32[]{:S(2)}) copy-start(f32[2,2,160,160]{3,2,1,0:T(8,128)} %param.24) | copy-start | bytes 1228804
Sparse Core Ops, SparseCore 0:
  9.5 26.0 all-gather.2
  197.3 26.3 all-gather.4
